TPU v7x, 32 devices: a whole 2x2x4 slice. The times are simulated.
32 devices in a mesh: fsdp: 16 (over z, x, core), dp: 2 (over y).
Axes of the slice: x: 2, y: 2, z: 4, core: 2. Of those that a mesh axis runs over, the one named last changes fastest.
Arguments:
- tokens: bfloat16 [24576, 1024], P(('fsdp', 'dp')), may hold values from -6 to 6
- cotangent: bfloat16 [24576, 1024], P(('fsdp', 'dp')), may hold values from -6 to 6
- segments: int32 [24576], replicated, may hold values from 0 to 47, never falling along the last dimension, each value on 1 to 577 neighbouring positions
- adapter_ids: int32 [48], replicated, may hold values from 0 to 7
- ln1_gain: float32 [1024], replicated, may hold values from 0.5 to 1.5
- ln1_bias: float32 [1024], replicated, may hold values from -1.5 to 1.5
- w_query: bfloat16 [1024, 1024], P(('fsdp', 'dp')), may hold values from -0.1875 to 0.1875
- b_query: float32 [1024], replicated, may hold values from -2.5 to 2.5
- w_key: bfloat16 [1024, 1024], P(('fsdp', 'dp')), may hold values from -0.1875 to 0.1875
- w_value: bfloat16 [1024, 1024], P(('fsdp', 'dp')), may hold values from -0.1875 to 0.1875
- b_value: float32 [1024], replicated, may hold values from -2.5 to 2.5
- w_out: bfloat16 [1024, 1024], P(('fsdp', 'dp')), may hold values from -4 to 4
- b_out: float32 [1024], replicated, may hold values from -2.5 to 2.5
- ln2_gain: float32 [1024], replicated, may hold values from 0.5 to 1.5
- ln2_bias: float32 [1024], replicated, may hold values from -1.5 to 1.5
- w_up: bfloat16 [1024, 4096], P(('fsdp', 'dp')), may hold values from -0.1875 to 0.1875
- b_up: float32 [4096], replicated, may hold values from -2.5 to 2.5
- w_down: bfloat16 [4096, 1024], P(('fsdp', 'dp')), may hold values from -0.1875 to 0.1875
- b_down: float32 [1024], replicated, may hold values from -2.5 to 2.5
- query_in: bfloat16 [1024, 128], P(('fsdp', 'dp')), may hold values from -0.1875 to 0.1875
- query_out: bfloat16 [1024, 128], P(('fsdp', 'dp')), may hold values from -0.75 to 0.75
- value_in: bfloat16 [1024, 128], P(('fsdp', 'dp')), may hold values from -0.1875 to 0.1875
- value_out: bfloat16 [1024, 128], P(('fsdp', 'dp')), may hold values from -0.75 to 0.75
- up_in: bfloat16 [1024, 128], P(('fsdp', 'dp')), may hold values from -0.1875 to 0.1875
- up_out: bfloat16 [4096, 128], P(('fsdp', 'dp')), may hold values from -0.75 to 0.75
- down_in: bfloat16 [4096, 128], P(('fsdp', 'dp')), may hold values from -0.1875 to 0.1875
- down_out: bfloat16 [1024, 128], P(('fsdp', 'dp')), may hold values from -0.75 to 0.75
Outputs:
- block_out: bfloat16 [24576, 1024], P(('fsdp', 'dp'))
- grad_input: bfloat16 [24576, 1024], P(('fsdp', 'dp'))
- grad_query_in: float32 [1024, 128], P(('fsdp', 'dp'))
- grad_query_out: float32 [1024, 128], P(('fsdp', 'dp'))
- grad_value_in: float32 [1024, 128], P(('fsdp', 'dp'))
- grad_value_out: float32 [1024, 128], P(('fsdp', 'dp'))
- grad_up_in: float32 [1024, 128], P(('fsdp', 'dp'))
- grad_up_out: float32 [4096, 128], P(('fsdp', 'dp'))
- grad_down_in: float32 [4096, 128], P(('fsdp', 'dp'))
- grad_down_out: float32 [1024, 128], P(('fsdp', 'dp'))
Inputs may be any that keep to these rules, and one draw needn't show every extreme that they name: `segments`: image numbers never fall along the packed order; each image holds 1 to 577 consecutive tokens, and one holds exactly 577.
All inputs are finite; a program needn't handle non-finite values.
Results may differ from a plain program's by a relative error of at most 0.014.
Values may be sent and summed in bfloat16 or wider, within the bound.
No kernel may reach another device: no remote copies, remote signals or barrier semaphores. Data moves between devices by JAX's collectives and lax.ppermute only.
A program may use at most 384 MiB of HBM per device.

v0:
```python
import jax
import jax.numpy as jnp
from jax import lax
from jax.sharding import PartitionSpec as P

HEADS = 16
HALO = 576
RANK = 16
ADAPTERS = 8
epsilon = 1e-05
gelu_slope = 1.702


def extended(array, sides, width):
    for axis, dim in sides:
        devices, length = (lax.axis_size(axis), array.shape[dim])
        up = [(i, (i + 1) % devices) for i in range(devices - 1)]
        down = [(j, i) for i, j in up]
        last = lax.slice_in_dim(array, length - width, length, axis=dim)
        first = lax.slice_in_dim(array, 0, width, axis=dim)
        before = lax.ppermute(last, axis, up)
        after = lax.ppermute(first, axis, down)
        array = jnp.concatenate([before, array, after], axis=dim)
    return array


def from_behind(value, axis, steps):
    count = lax.axis_size(axis)
    first, last = (max(0, -steps), min(count, count - steps))
    return lax.ppermute(value, axis, [(source, source + steps) for source in range(first, last)])


def product(left, right):
    return jnp.dot(left, right, preferred_element_type=jnp.float32)


def times_transposed(left, right):
    return lax.dot_general(
        left, right, (((1,), (1,)), ((), ())), preferred_element_type=jnp.float32
    )


def transposed_times(left, right):
    return lax.dot_general(
        left, right, (((0,), (0,)), ((), ())), preferred_element_type=jnp.float32
    )


def norm_forward(values, gain, shift):
    mean = jnp.mean(values, axis=1, keepdims=True)
    centered = values - mean
    inverse = lax.rsqrt(jnp.mean(centered * centered, axis=1, keepdims=True) + epsilon)
    normed = centered * inverse
    return (normed * gain + shift, normed, inverse)


def norm_backward(grad, normed, inverse, gain):
    scaled = grad * gain
    return inverse * (
        scaled
        - jnp.mean(scaled, axis=1, keepdims=True)
        - normed * jnp.mean(scaled * normed, axis=1, keepdims=True)
    )


def split_heads(block, head_dim):
    return block.reshape(block.shape[0], block.shape[1] // head_dim, head_dim)


def group_scores(query3, key3, same_image, score_scale):
    raw = jnp.einsum("qhd,khd->hqk", query3, key3, preferred_element_type=jnp.float32) * score_scale
    return jnp.where(same_image[None], raw, -1000000000.0)


def local(
    tokens,
    cotangent,
    segments,
    adapter_ids,
    ln1_gain,
    ln1_bias,
    w_query,
    b_query,
    w_key,
    w_value,
    b_value,
    w_out,
    b_out,
    ln2_gain,
    ln2_bias,
    w_up,
    b_up,
    w_down,
    b_down,
    query_in,
    query_out,
    value_in,
    value_out,
    up_in,
    up_out,
    down_in,
    down_out,
):
    row_count, model_width = tokens.shape
    head_dim = model_width // HEADS
    score_scale = head_dim ** (-0.5)
    group_count = max(1, HEADS // 4)
    group_width = model_width // group_count
    gathered = (
        lax.all_gather(w_query, ("fsdp", "dp"), axis=0, tiled=True),
        lax.all_gather(w_key, ("fsdp", "dp"), axis=0, tiled=True),
        lax.all_gather(w_value, ("fsdp", "dp"), axis=0, tiled=True),
        lax.all_gather(w_out, ("fsdp", "dp"), axis=0, tiled=True),
        lax.all_gather(w_up, ("fsdp", "dp"), axis=0, tiled=True),
        lax.all_gather(w_down, ("fsdp", "dp"), axis=0, tiled=True),
        lax.all_gather(query_in, ("fsdp", "dp"), axis=0, tiled=True),
        lax.all_gather(query_out, ("fsdp", "dp"), axis=0, tiled=True),
        lax.all_gather(value_in, ("fsdp", "dp"), axis=0, tiled=True),
        lax.all_gather(value_out, ("fsdp", "dp"), axis=0, tiled=True),
        lax.all_gather(up_in, ("fsdp", "dp"), axis=0, tiled=True),
        lax.all_gather(up_out, ("fsdp", "dp"), axis=0, tiled=True),
        lax.all_gather(down_in, ("fsdp", "dp"), axis=0, tiled=True),
        lax.all_gather(down_out, ("fsdp", "dp"), axis=0, tiled=True),
    )
    (
        full_wq,
        full_wk,
        full_wv,
        full_wo,
        full_wup,
        full_wdown,
        full_qin,
        full_qout,
        full_vin,
        full_vout,
        full_uin,
        full_uout,
        full_din,
        full_dout,
    ) = gathered
    position = lax.axis_index(("fsdp", "dp"))
    padded_seg = jnp.pad(segments, HALO, constant_values=-1)
    seg_window = lax.dynamic_slice_in_dim(padded_seg, position * row_count, row_count + 2 * HALO, 0)
    seg_own = lax.dynamic_slice_in_dim(segments, position * row_count, row_count, 0)
    same_image = seg_own[:, None] == seg_window[None, :]
    image_hot = (
        seg_own[:, None] == jnp.arange(adapter_ids.shape[0], dtype=jnp.int32)[None, :]
    ).astype(jnp.bfloat16)
    adapter_hot = (adapter_ids[:, None] == jnp.arange(ADAPTERS, dtype=jnp.int32)[None, :]).astype(
        jnp.bfloat16
    )
    select = jnp.repeat(product(image_hot, adapter_hot), RANK, axis=1).astype(jnp.bfloat16)
    tokens_f = tokens.astype(jnp.float32)
    normal1, hat_one, inv_one = norm_forward(tokens_f, ln1_gain, ln1_bias)
    normed1 = normal1.astype(jnp.bfloat16)
    low_q = product(normed1, full_qin).astype(jnp.bfloat16) * select
    low_v = product(normed1, full_vin).astype(jnp.bfloat16) * select
    query = (product(normed1, full_wq) + b_query + times_transposed(low_q, full_qout)).astype(
        jnp.bfloat16
    )
    keys = product(normed1, full_wk).astype(jnp.bfloat16)
    values = (product(normed1, full_wv) + b_value + times_transposed(low_v, full_vout)).astype(
        jnp.bfloat16
    )
    window = extended(jnp.concatenate([keys, values], axis=1), ((("fsdp", "dp"), 0),), HALO)
    key_window = window[:, :model_width]
    value_window = window[:, model_width:]
    mixed_parts = []
    log_totals = []
    for head_group in range(group_count):
        first = head_group * group_width
        query3 = split_heads(query[:, first : first + group_width], head_dim)
        key3 = split_heads(key_window[:, first : first + group_width], head_dim)
        value3 = split_heads(value_window[:, first : first + group_width], head_dim)
        scores = group_scores(query3, key3, same_image, score_scale)
        row_max = jnp.max(scores, axis=2, keepdims=True)
        exp_scores = jnp.exp(scores - row_max)
        row_total = jnp.sum(exp_scores, axis=2, keepdims=True)
        softmax_w = (exp_scores / row_total).astype(jnp.bfloat16)
        log_totals.append(row_max + jnp.log(row_total))
        attended = jnp.einsum("hqk,khd->qhd", softmax_w, value3, preferred_element_type=jnp.float32)
        mixed_parts.append(attended.reshape(row_count, group_width))
    mixed = jnp.concatenate(mixed_parts, axis=1).astype(jnp.bfloat16)
    resid = tokens_f + product(mixed, full_wo) + b_out
    normal2, hat_two, inv_two = norm_forward(resid, ln2_gain, ln2_bias)
    normed2 = normal2.astype(jnp.bfloat16)
    low_u = product(normed2, full_uin).astype(jnp.bfloat16) * select
    pre_act = product(normed2, full_wup) + b_up + times_transposed(low_u, full_uout)
    gate_value = 1.0 / (1.0 + jnp.exp(-gelu_slope * pre_act))
    act = (pre_act * gate_value).astype(jnp.bfloat16)
    low_d = product(act, full_din).astype(jnp.bfloat16) * select
    result = resid + product(act, full_wdown) + b_down + times_transposed(low_d, full_dout)
    block_out = result.astype(jnp.bfloat16)
    again = (
        lax.all_gather(w_query, ("fsdp", "dp"), axis=0, tiled=True),
        lax.all_gather(w_key, ("fsdp", "dp"), axis=0, tiled=True),
        lax.all_gather(w_value, ("fsdp", "dp"), axis=0, tiled=True),
        lax.all_gather(w_out, ("fsdp", "dp"), axis=0, tiled=True),
        lax.all_gather(w_up, ("fsdp", "dp"), axis=0, tiled=True),
        lax.all_gather(w_down, ("fsdp", "dp"), axis=0, tiled=True),
        lax.all_gather(query_in, ("fsdp", "dp"), axis=0, tiled=True),
        lax.all_gather(query_out, ("fsdp", "dp"), axis=0, tiled=True),
        lax.all_gather(value_in, ("fsdp", "dp"), axis=0, tiled=True),
        lax.all_gather(value_out, ("fsdp", "dp"), axis=0, tiled=True),
        lax.all_gather(up_in, ("fsdp", "dp"), axis=0, tiled=True),
        lax.all_gather(up_out, ("fsdp", "dp"), axis=0, tiled=True),
        lax.all_gather(down_in, ("fsdp", "dp"), axis=0, tiled=True),
        lax.all_gather(down_out, ("fsdp", "dp"), axis=0, tiled=True),
    )
    (
        back_wq,
        back_wk,
        back_wv,
        back_wo,
        back_wup,
        back_wdown,
        back_qin,
        back_qout,
        back_vin,
        back_vout,
        back_uin,
        back_uout,
        back_din,
        back_dout,
    ) = again
    grad_down_out = transposed_times(cotangent, low_d)
    d_low_d = product(cotangent, back_dout).astype(jnp.bfloat16) * select
    grad_down_in = transposed_times(act, d_low_d)
    d_act = times_transposed(cotangent, back_wdown) + times_transposed(d_low_d, back_din)
    d_pre = (d_act * (gate_value + gelu_slope * pre_act * gate_value * (1.0 - gate_value))).astype(
        jnp.bfloat16
    )
    grad_up_out = transposed_times(d_pre, low_u)
    d_low_u = product(d_pre, back_uout).astype(jnp.bfloat16) * select
    grad_up_in = transposed_times(normed2, d_low_u)
    d_normed2 = times_transposed(d_pre, back_wup) + times_transposed(d_low_u, back_uin)
    d_resid = cotangent.astype(jnp.float32) + norm_backward(d_normed2, hat_two, inv_two, ln2_gain)
    d_attn = d_resid.astype(jnp.bfloat16)
    d_mixed = times_transposed(d_attn, back_wo).astype(jnp.bfloat16)
    query_grads = []
    key_grads = []
    value_grads = []
    for head_group in range(group_count):
        first = head_group * group_width
        query3 = split_heads(query[:, first : first + group_width], head_dim)
        key3 = split_heads(key_window[:, first : first + group_width], head_dim)
        value3 = split_heads(value_window[:, first : first + group_width], head_dim)
        d_out3 = split_heads(d_mixed[:, first : first + group_width], head_dim)
        scores = group_scores(query3, key3, same_image, score_scale)
        exact_probs = jnp.exp(scores - log_totals[head_group])
        softmax_w = exact_probs.astype(jnp.bfloat16)
        d_probs = jnp.einsum("qhd,khd->hqk", d_out3, value3, preferred_element_type=jnp.float32)
        row_delta = jnp.sum(exact_probs * d_probs, axis=2, keepdims=True)
        d_scores = (exact_probs * (d_probs - row_delta)).astype(jnp.bfloat16)
        grad_q3 = (
            jnp.einsum("hqk,khd->qhd", d_scores, key3, preferred_element_type=jnp.float32)
            * score_scale
        )
        grad_k3 = (
            jnp.einsum("hqk,qhd->khd", d_scores, query3, preferred_element_type=jnp.float32)
            * score_scale
        )
        grad_v3 = jnp.einsum("hqk,qhd->khd", softmax_w, d_out3, preferred_element_type=jnp.float32)
        query_grads.append(grad_q3.reshape(row_count, group_width))
        key_grads.append(grad_k3.reshape(grad_k3.shape[0], group_width))
        value_grads.append(grad_v3.reshape(grad_v3.shape[0], group_width))
    d_query = jnp.concatenate(query_grads, axis=1).astype(jnp.bfloat16)
    d_kv_window = jnp.concatenate(key_grads + value_grads, axis=1)
    from_right = from_behind(d_kv_window[:HALO].astype(jnp.bfloat16), ("fsdp", "dp"), -1).astype(
        jnp.float32
    )
    from_left = from_behind(
        d_kv_window[row_count + HALO :].astype(jnp.bfloat16), ("fsdp", "dp"), 1
    ).astype(jnp.float32)
    d_kv_own = d_kv_window[HALO : HALO + row_count]
    d_kv_own = (
        d_kv_own
        + jnp.pad(from_left, ((0, row_count - HALO), (0, 0)))
        + jnp.pad(from_right, ((row_count - HALO, 0), (0, 0)))
    )
    d_keys = d_kv_own[:, :model_width].astype(jnp.bfloat16)
    d_values = d_kv_own[:, model_width:].astype(jnp.bfloat16)
    grad_query_out = transposed_times(d_query, low_q)
    grad_value_out = transposed_times(d_values, low_v)
    d_low_q = product(d_query, back_qout).astype(jnp.bfloat16) * select
    d_low_v = product(d_values, back_vout).astype(jnp.bfloat16) * select
    grad_query_in = transposed_times(normed1, d_low_q)
    grad_value_in = transposed_times(normed1, d_low_v)
    d_normed1 = (
        times_transposed(d_query, back_wq)
        + times_transposed(d_keys, back_wk)
        + times_transposed(d_values, back_wv)
    )
    d_normed1 = (
        d_normed1 + times_transposed(d_low_q, back_qin) + times_transposed(d_low_v, back_vin)
    )
    grad_input = (d_resid + norm_backward(d_normed1, hat_one, inv_one, ln1_gain)).astype(
        jnp.bfloat16
    )
    summed = (
        lax.psum_scatter(grad_query_in, ("fsdp", "dp"), scatter_dimension=0, tiled=True),
        lax.psum_scatter(grad_query_out, ("fsdp", "dp"), scatter_dimension=0, tiled=True),
        lax.psum_scatter(grad_value_in, ("fsdp", "dp"), scatter_dimension=0, tiled=True),
        lax.psum_scatter(grad_value_out, ("fsdp", "dp"), scatter_dimension=0, tiled=True),
        lax.psum_scatter(grad_up_in, ("fsdp", "dp"), scatter_dimension=0, tiled=True),
        lax.psum_scatter(grad_up_out, ("fsdp", "dp"), scatter_dimension=0, tiled=True),
        lax.psum_scatter(grad_down_in, ("fsdp", "dp"), scatter_dimension=0, tiled=True),
        lax.psum_scatter(grad_down_out, ("fsdp", "dp"), scatter_dimension=0, tiled=True),
    )
    return (
        block_out,
        grad_input,
        summed[0],
        summed[1],
        summed[2],
        summed[3],
        summed[4],
        summed[5],
        summed[6],
        summed[7],
    )


def solution(mesh):
    return jax.shard_map(
        local,
        mesh=mesh,
        in_specs=(
            P(("fsdp", "dp"), None),
            P(("fsdp", "dp"), None),
            P(),
            P(),
            P(),
            P(),
            P(("fsdp", "dp"), None),
            P(),
            P(("fsdp", "dp"), None),
            P(("fsdp", "dp"), None),
            P(),
            P(("fsdp", "dp"), None),
            P(),
            P(),
            P(),
            P(("fsdp", "dp"), None),
            P(),
            P(("fsdp", "dp"), None),
            P(),
            P(("fsdp", "dp"), None),
            P(("fsdp", "dp"), None),
            P(("fsdp", "dp"), None),
            P(("fsdp", "dp"), None),
            P(("fsdp", "dp"), None),
            P(("fsdp", "dp"), None),
            P(("fsdp", "dp"), None),
            P(("fsdp", "dp"), None),
        ),
        out_specs=(
            P(("fsdp", "dp"), None),
            P(("fsdp", "dp"), None),
            P(("fsdp", "dp"), None),
            P(("fsdp", "dp"), None),
            P(("fsdp", "dp"), None),
            P(("fsdp", "dp"), None),
            P(("fsdp", "dp"), None),
            P(("fsdp", "dp"), None),
            P(("fsdp", "dp"), None),
            P(("fsdp", "dp"), None),
        ),
        check_vma=False,
    )
```

profile of v0, /device:TPU:0, one launch (start us, length us, event | category | flops | bytes accessed | tf_op | source)
XLA Modules:
  0.0 2053.9 jit_solution(11524287528089910341)
XLA Ops:
  16.4 76.2 %all_gather.61 = bf16[1024,128]{1,0:T(8,128)(2,1)} all-gather(bf16[32,128]{1,0:T(8,128)(2,1)S(1)} %copy-done.96), channel_id=1, replica_groups=mesh['fsdp'=16,'dp'=2] {'fsdp','dp'}, dimensions={0}, use_global_device_ids=true | all-gather | bytes 270336 | tf_op jit(solution)/shard_map/all_gather | solution.py:116
  92.6 70.0 %all_gather.62 = bf16[1024,128]{1,0:T(8,128)(2,1)} all-gather(bf16[32,128]{1,0:T(8,128)(2,1)S(1)} %copy-done.97), channel_id=1, replica_groups=mesh['fsdp'=16,'dp'=2] {'fsdp','dp'}, dimensions={0}, use_global_device_ids=true | all-gather | bytes 270336 | tf_op jit(solution)/shard_map/all_gather | solution.py:117
  162.6 67.6 %all_gather.58 = bf16[1024,128]{1,0:T(8,128)(2,1)S(1)} all-gather(bf16[32,128]{1,0:T(8,128)(2,1)S(1)} %copy-done.98), channel_id=1, replica_groups=mesh['fsdp'=16,'dp'=2] {'fsdp','dp'}, dimensions={0}, use_global_device_ids=true | all-gather | bytes 270336 | tf_op jit(solution)/shard_map/all_gather | solution.py:118
  230.2 70.7 %all_gather.59 = bf16[1024,128]{1,0:T(8,128)(2,1)} all-gather(bf16[32,128]{1,0:T(8,128)(2,1)S(1)} %copy-done.99), channel_id=1, replica_groups=mesh['fsdp'=16,'dp'=2] {'fsdp','dp'}, dimensions={0}, use_global_device_ids=true | all-gather | bytes 270336 | tf_op jit(solution)/shard_map/all_gather | solution.py:119
  300.9 73.3 %all_gather.65 = bf16[1024,128]{1,0:T(8,128)(2,1)} all-gather(bf16[32,128]{1,0:T(8,128)(2,1)S(1)} %copy-done.100), channel_id=1, replica_groups=mesh['fsdp'=16,'dp'=2] {'fsdp','dp'}, dimensions={0}, use_global_device_ids=true | all-gather | bytes 270336 | tf_op jit(solution)/shard_map/all_gather | solution.py:120
  394.6 160.8 %all_gather.69 = bf16[1024,128]{1,0:T(8,128)(2,1)S(1)} all-gather(bf16[32,128]{1,0:T(8,128)(2,1)S(1)} %copy-done.101), channel_id=1, replica_groups=mesh['fsdp'=16,'dp'=2] {'fsdp','dp'}, dimensions={0}, use_global_device_ids=true | all-gather | bytes 270336 | tf_op jit(solution)/shard_map/all_gather | solution.py:123
  595.0 11.6 fusion.90
  606.7 10.1 fusion.1
  617.4 10.1 fusion.53
  627.6 10.3 fusion.89
  637.9 10.1 fusion.2
  648.6 11.2 fusion.52
  659.8 10.5 fusion.88
  670.2 10.1 fusion.3
  681.0 10.8 fusion.51
  691.8 10.4 fusion.91
  702.2 10.1 fusion
  712.9 10.9 fusion.54
  732.0 12.3 fusion.97
  744.3 12.1 fusion.95
  756.5 13.5 multiply_convert_fusion.5
  769.9 11.2 multiply_convert_fusion.4
  785.2 11.0 fusion.98
  801.8 11.1 fusion.8
  813.0 18.6 multiply_reduce_fusion
  831.5 15.7 multiply_convert_fusion
  853.8 11.2 fusion.10
  865.0 18.8 multiply_reduce_fusion.1
  884.0 11.1 fusion.12
  895.1 18.6 multiply_reduce_fusion.2
  913.9 11.2 fusion.14
  925.1 18.6 multiply_reduce_fusion.3
  957.4 15.7 multiply_convert_fusion.1
  979.3 15.7 multiply_convert_fusion.2
  1001.1 15.8 multiply_convert_fusion.3
  1037.0 9.8 convert.60
  1064.1 8.0 fusion.57
  1072.2 8.1 fusion.56
  1080.4 8.1 fusion.55
  1093.9 48.1 %collective-permute-done.2 = bf16[576,2048]{1,0:T(8,128)(2,1)} collective-permute-done((bf16[576,2048]{1,0:T(8,128)(2,1)}, bf16[576,2048]{1,0:T(8,128)(2,1)}, u32[]{:S(2)}, u32[]{:S(2)}) %collective-permute-start.2) | collective-permute-done | bytes 2359328 | tf_op jit(solution)/shard_map/ppermute | solution.py:30
  1167.3 11.0 fusion.96
  1193.1 41.3 %reduce-scatter.25.cloned.1.call-done = f32[32,128]{1,0:T(8,128)} async-done(((f32[1024,128]{1,0:T(8,128)}), f32[32,128]{1,0:T(8,128)}) %reduce-scatter.25.cloned.1.call-update) | async-done | bytes 16400
  1234.4 134.7 %reduce-scatter.13.cloned.1.call-done = f32[32,128]{1,0:T(8,128)} async-done(((f32[1024,128]{1,0:T(8,128)}), f32[32,128]{1,0:T(8,128)}) %reduce-scatter.13.cloned.1.call-update) | async-done | bytes 16400 | tf_op jit(solution)/shard_map/reduce_scatter | solution.py:302
  1369.1 134.3 %reduce-scatter.11.cloned.1.call-done = f32[32,128]{1,0:T(8,128)} async-done(((f32[1024,128]{1,0:T(8,128)}), f32[32,128]{1,0:T(8,128)}) %reduce-scatter.11.cloned.1.call-update) | async-done | bytes 16400 | tf_op jit(solution)/shard_map/reduce_scatter | solution.py:301
  1503.4 134.5 %reduce-scatter.15.cloned.1.call-done = f32[32,128]{1,0:T(8,128)} async-done(((f32[1024,128]{1,0:T(8,128)}), f32[32,128]{1,0:T(8,128)}) %reduce-scatter.15.cloned.1.call-update) | async-done | bytes 16400 | tf_op jit(solution)/shard_map/reduce_scatter | solution.py:303
  1637.9 134.3 %reduce-scatter.17.cloned.1.call-done = f32[32,128]{1,0:T(8,128)} async-done(((f32[1024,128]{1,0:T(8,128)}), f32[32,128]{1,0:T(8,128)}) %reduce-scatter.17.cloned.1.call-update) | async-done | bytes 16400 | tf_op jit(solution)/shard_map/reduce_scatter | solution.py:304
  1772.2 137.1 %reduce-scatter.21.cloned.1.call-done = f32[128,128]{1,0:T(8,128)} async-done(((f32[4096,128]{1,0:T(8,128)}), f32[128,128]{1,0:T(8,128)}) %reduce-scatter.21.cloned.1.call-update) | async-done | bytes 65552 | tf_op jit(solution)/shard_map/reduce_scatter | solution.py:306
  1909.3 137.8 %reduce-scatter.23.cloned.1.call-done = f32[128,128]{1,0:T(8,128)} async-done(((f32[4096,128]{1,0:T(8,128)}), f32[128,128]{1,0:T(8,128)}) %reduce-scatter.23.cloned.1.call-update) | async-done | bytes 65552 | tf_op jit(solution)/shard_map/reduce_scatter | solution.py:307
  (375 shorter events, 204.0 us)
Async XLA Ops:
  7.2 85.4 %copy-start.97 = (bf16[32,128]{1,0:T(8,128)(2,1)S(1)}, bf16[32,128]{1,0:T(8,128)(2,1)}, u32[]{:S(2)}) copy-start(bf16[32,128]{1,0:T(8,128)(2,1)} %param.47) | copy-start | bytes 24580
  7.2 155.4 %copy-start.98 = (bf16[32,128]{1,0:T(8,128)(2,1)S(1)}, bf16[32,128]{1,0:T(8,128)(2,1)}, u32[]{:S(2)}) copy-start(bf16[32,128]{1,0:T(8,128)(2,1)} %param.48) | copy-start | bytes 24580
  7.2 223.0 %copy-start.99 = (bf16[32,128]{1,0:T(8,128)(2,1)S(1)}, bf16[32,128]{1,0:T(8,128)(2,1)}, u32[]{:S(2)}) copy-start(bf16[32,128]{1,0:T(8,128)(2,1)} %param.49) | copy-start | bytes 24580
  7.2 293.7 %copy-start.100 = (bf16[32,128]{1,0:T(8,128)(2,1)S(1)}, bf16[32,128]{1,0:T(8,128)(2,1)}, u32[]{:S(2)}) copy-start(bf16[32,128]{1,0:T(8,128)(2,1)} %param.50) | copy-start | bytes 24580
  7.2 367.0 %copy-start.94 = (f32[1024]{0:T(1024)S(1)}, f32[1024]{0:T(1024)}, u32[]{:S(2)}) copy-start(f32[1024]{0:T(1024)} %param.31) | copy-start | bytes 12292
  7.3 366.9 %copy-start.102 = (f32[1024]{0:T(1024)S(1)}, f32[1024]{0:T(1024)}, u32[]{:S(2)}) copy-start(f32[1024]{0:T(1024)} %param.32) | copy-start | bytes 12292
  7.3 368.2 %all-gather.11.cloned.1.call-start = ((), (), s32[]{:S(2)}) async-start(), calls=%async_computation.9 | async-start | bytes 2162688 | tf_op jit(solution)/shard_map/all_gather | solution.py:112
  8.0 372.3 %all-gather.9.cloned.1.call-start = ((), (), s32[]{:S(2)}) async-start(), calls=%async_computation.8 | async-start | bytes 2162688 | tf_op jit(solution)/shard_map/all_gather | solution.py:111
  8.8 550.1 %all-gather.13.cloned.1.call-start = ((), (), s32[]{:S(2)}) async-start(), calls=%async_computation.10 | async-start | bytes 2162688 | tf_op jit(solution)/shard_map/all_gather | solution.py:110
  9.5 714.4 %all-gather.15.cloned.1.call-start = ((), (), s32[]{:S(2)}) async-start(), calls=%async_computation.11 | async-start | bytes 2162688 | tf_op jit(solution)/shard_map/all_gather | solution.py:113
  10.1 722.0 %all-gather.21.cloned.1.call-start = ((), (), s32[]{:S(2)}) async-start(), calls=%async_computation.14 | async-start | bytes 8650752 | tf_op jit(solution)/shard_map/all_gather | solution.py:115
  10.7 733.7 %all-gather.17.cloned.1.call-start = ((), (), s32[]{:S(2)}) async-start(), calls=%async_computation.12 | async-start | bytes 8650752 | tf_op jit(solution)/shard_map/all_gather | solution.py:114
  11.2 745.2 %all-gather.19.cloned.1.call-start = ((), (), s32[]{:S(2)}) async-start(), calls=%async_computation.13 | async-start | bytes 1081344 | tf_op jit(solution)/shard_map/all_gather | solution.py:121
  12.0 758.0 %all-gather.23.cloned.1.call-start = ((), (), s32[]{:S(2)}) async-start(), calls=%async_computation.15 | async-start | bytes 1081344 | tf_op jit(solution)/shard_map/all_gather | solution.py:122
  12.7 1180.4 %reduce-scatter.19.cloned.1.call-start = ((), (), s32[]{:S(2)}) async-start(), calls=%async_computation.20 | async-start | bytes 540672 | tf_op jit(solution)/shard_map/reduce_scatter | solution.py:305
  14.5 359.7 %copy-start.89 = (f32[768]{0:T(1024)}, f32[768]{0:T(1024)S(1)}, u32[]{:S(2)}) copy-start(f32[768]{0:T(1024)S(1)} %broadcast_multiply_fusion.5) | copy-start | bytes 9220
  15.1 359.1 %copy-start.91 = (f32[768]{0:T(1024)}, f32[768]{0:T(1024)S(1)}, u32[]{:S(2)}) copy-start(f32[768]{0:T(1024)S(1)} %add_rsqrt_fusion.1) | copy-start | bytes 9220
  16.4 540.3 %copy-start.45 = (bf16[768,128]{1,0:T(8,128)(2,1)}, bf16[768,128]{1,0:T(8,128)(2,1)S(1)}, u32[]{:S(2)}) copy-start(bf16[768,128]{1,0:T(8,128)(2,1)S(1)} %copy.96) | copy-start | bytes 589828
  230.2 144.6 %copy-start.55 = (bf16[1024,128]{1,0:T(8,128)(2,1)}, bf16[1024,128]{1,0:T(8,128)(2,1)S(1)}, u32[]{:S(2)}) copy-start(bf16[1024,128]{1,0:T(8,128)(2,1)S(1)} %all_gather.58) | copy-start | bytes 786436
  374.9 184.0 %copy-start.7 = (bf16[768,1024]{1,0:T(8,128)(2,1)}, bf16[768,1024]{1,0:T(8,128)(2,1)S(1)}, u32[]{:S(2)}) copy-start(bf16[768,1024]{1,0:T(8,128)(2,1)S(1)} %fusion.32) | copy-start | bytes 4718596
  384.3 171.1 %copy-start.57 = (bf16[1024,128]{1,0:T(8,128)(2,1)S(1)}, bf16[1024,128]{1,0:T(8,128)(2,1)}, u32[]{:S(2)}) copy-start(bf16[1024,128]{1,0:T(8,128)(2,1)} %all_gather.61) | copy-start | bytes 786436
  384.3 172.4 %copy-start.19 = (bf16[768,1024]{1,0:T(8,128)(2,1)S(1)}, bf16[768,1024]{1,0:T(8,128)(2,1)}, u32[]{:S(2)}) copy-start(bf16[768,1024]{1,0:T(8,128)(2,1)} %param.28) | copy-start | bytes 4718596
  390.5 180.3 %collective-permute-start = (bf16[576,2048]{1,0:T(8,128)(2,1)}, bf16[576,2048]{1,0:T(8,128)(2,1)}, u32[]{:S(2)}, u32[]{:S(2)}) collective-permute-start(bf16[576,2048]{1,0:T(8,128)(2,1)} %get-tuple-element.54), channel_id=1, source_target_pairs={{0,1},{1,2},{2,3},{3,4},{4,5},{5,6},{6,7},{7,8},{8,9},{9,10},{10,1... | collective-permute-start | bytes 7077896 | tf_op jit(solution)/shard_map/ppermute | solution.py:21
  393.2 177.6 %collective-permute-start.1 = (bf16[576,2048]{1,0:T(8,128)(2,1)}, bf16[576,2048]{1,0:T(8,128)(2,1)}, u32[]{:S(2)}, u32[]{:S(2)}) collective-permute-start(bf16[576,2048]{1,0:T(8,128)(2,1)} %get-tuple-element.55), channel_id=1, source_target_pairs={{1,0},{2,1},{3,2},{4,3},{5,4},{6,5},{7,6},{8,7},{9,8},{10,9},{11,1... | collective-permute-start | bytes 7077896 | tf_op jit(solution)/shard_map/ppermute | solution.py:22
  580.1 111.7 %copy-start.9 = (bf16[1920,256]{0,1:T(8,128)(2,1)}, bf16[1920,256]{0,1:T(8,128)(2,1)S(1)}, u32[]{:S(2)}) copy-start(bf16[1920,256]{0,1:T(8,128)(2,1)S(1)} %copy.100) | copy-start | bytes 2949124
  590.2 16.5 copy-start.11
  648.6 11.2 copy-start.53
  728.3 69.2 %copy-start.3 = (f32[768,1024]{1,0:T(8,128)}, f32[768,1024]{1,0:T(8,128)S(1)}, u32[]{:S(2)}) copy-start(f32[768,1024]{1,0:T(8,128)S(1)} %get-tuple-element.73) | copy-start | bytes 9437188
  756.5 13.5 copy-start.79
  769.9 11.2 copy-start.111
  831.5 15.7 copy-start.16
  865.0 19.0 copy-start.84
  895.1 18.8 copy-start.85
  913.9 11.2 copy-start.38
  943.7 290.6 %reduce-scatter.25.cloned.1.call-start = ((), (), s32[]{:S(2)}) async-start(), calls=%async_computation.23 | async-start | bytes 540672
  957.4 15.8 copy-start.52
  979.3 15.7 copy-start.50
  1001.1 15.8 copy-start.49
  1058.4 83.6 %collective-permute-start.2 = (bf16[576,2048]{1,0:T(8,128)(2,1)}, bf16[576,2048]{1,0:T(8,128)(2,1)}, u32[]{:S(2)}, u32[]{:S(2)}) collective-permute-start(bf16[576,2048]{1,0:T(8,128)(2,1)} %get-tuple-element.44), channel_id=1, source_target_pairs={{0,1},{1,2},{2,3},{3,4},{4,5},{5,6},{6,7},{7,8},{8,9},{9,10},{10,1... | collective-permute-start | bytes 7077896 | tf_op jit(solution)/shard_map/ppermute | solution.py:30
  1062.7 80.0 %collective-permute-start.3 = (bf16[576,2048]{1,0:T(8,128)(2,1)}, bf16[576,2048]{1,0:T(8,128)(2,1)}, u32[]{:S(2)}, u32[]{:S(2)}) collective-permute-start(bf16[576,2048]{1,0:T(8,128)(2,1)} %get-tuple-element.45), channel_id=1, source_target_pairs={{1,0},{2,1},{3,2},{4,3},{5,4},{6,5},{7,6},{8,7},{9,8},{10,9},{11,1... | collective-permute-start | bytes 7077896 | tf_op jit(solution)/shard_map/ppermute | solution.py:30
  1072.2 296.9 %reduce-scatter.13.cloned.1.call-start = ((), (), s32[]{:S(2)}) async-start(), calls=%async_computation.17 | async-start | bytes 540672 | tf_op jit(solution)/shard_map/reduce_scatter | solution.py:302
  1089.9 413.5 %reduce-scatter.11.cloned.1.call-start = ((), (), s32[]{:S(2)}) async-start(), calls=%async_computation.16 | async-start | bytes 540672 | tf_op jit(solution)/shard_map/reduce_scatter | solution.py:301
  1093.8 55.6 %copy-start.65 = (bf16[1024,128]{1,0:T(8,128)(2,1)S(1)}, bf16[1024,128]{1,0:T(8,128)(2,1)}, u32[]{:S(2)}) copy-start(bf16[1024,128]{1,0:T(8,128)(2,1)} %all_gather.59) | copy-start | bytes 786436
  1093.8 544.1 %reduce-scatter.15.cloned.1.call-start = ((), (), s32[]{:S(2)}) async-start(), calls=%async_computation.18 | async-start | bytes 540672 | tf_op jit(solution)/shard_map/reduce_scatter | solution.py:303
  1152.1 620.1 %reduce-scatter.17.cloned.1.call-start = ((), (), s32[]{:S(2)}) async-start(), calls=%async_computation.19 | async-start | bytes 540672 | tf_op jit(solution)/shard_map/reduce_scatter | solution.py:304
  1155.0 754.3 %reduce-scatter.21.cloned.1.call-start = ((), (), s32[]{:S(2)}) async-start(), calls=%async_computation.21 | async-start | bytes 2162688 | tf_op jit(solution)/shard_map/reduce_scatter | solution.py:306
  1161.1 886.1 %reduce-scatter.23.cloned.1.call-start = ((), (), s32[]{:S(2)}) async-start(), calls=%async_computation.22 | async-start | bytes 2162688 | tf_op jit(solution)/shard_map/reduce_scatter | solution.py:307
  1167.3 11.6 copy-start.104
  (86 other events, 426.3 us)
Sparse Core Ops, SparseCore 0:
  11.2 59.3 all-gather.10
  73.7 55.3 all-gather.8
  132.2 55.6 all-gather.12
  190.8 55.3 all-gather.14
  249.2 77.4 all-gather.20
  329.6 112.4 all-gather.16
  445.0 55.7 all-gather.18
  503.6 52.7 all-gather.22
  943.9 150.1 reduce-scatter.18
  1096.7 137.6 reduce-scatter.24
  1237.2 131.8 reduce-scatter.12
  1371.8 131.6 reduce-scatter.10
  1506.2 131.6 reduce-scatter.14
  1640.6 131.6 reduce-scatter.16
  1774.9 134.3 reduce-scatter.20
  1912.0 135.1 reduce-scatter.22
where the time goes:
time: 2060 us; the launch traced here: 2050 us
  waiting for transfers between devices  908 us (44%)
  blocking collectives  519 us (25%)
  matrix products  376 us (18%)
  other arithmetic  140 us (7%)
  local copies, waits for them, and re-layouts  84.7 us (4%)
    all_gather x1, blocking collectives, local(): lax.all_gather(down_out, ('fsdp', 'dp'), axis=0, tiled=True)  161 us
    reduce_scatter x1, waiting for transfers between devices, local(): lax.psum_scatter(grad_down_in, ('fsdp', 'dp'), scatter_dimension=0, tiled...  138 us
    reduce_scatter x1, waiting for transfers between devices, local(): lax.psum_scatter(grad_up_out, ('fsdp', 'dp'), scatter_dimension=0, tiled=...  137 us
    reduce_scatter x1, waiting for transfers between devices, local(): lax.psum_scatter(grad_query_out, ('fsdp', 'dp'), scatter_dimension=0, til...  135 us
    reduce_scatter x1, waiting for transfers between devices, local(): lax.psum_scatter(grad_value_in, ('fsdp', 'dp'), scatter_dimension=0, tile...  135 us
    reduce_scatter x1, waiting for transfers between devices, local(): lax.psum_scatter(grad_value_out, ('fsdp', 'dp'), scatter_dimension=0, til...  134 us
    reduce_scatter x1, waiting for transfers between devices, local(): lax.psum_scatter(grad_query_in, ('fsdp', 'dp'), scatter_dimension=0, tile...  134 us
    all_gather x1, blocking collectives, local(): lax.all_gather(query_in, ('fsdp', 'dp'), axis=0, tiled=True)  76.2 us
  transfers between devices with their start and end apart: 20, of which 9 were waited for; matrix products, arithmetic and copies ran while one was open for 20% of the time, Pallas kernels for 0%

commit v1 on v0

--- a/solution.py
+++ b/solution.py
@@ -1,3 +1,4 @@
+import functools
 import jax
 import jax.numpy as jnp
 from jax import lax
@@ -9,6 +10,35 @@
 ADAPTERS = 8
 epsilon = 1e-05
 gelu_slope = 1.702
+
+
+def fix_levels_all(slab_in, row_dim):
+    vec_out = list(slab_in.shape[1:])
+    vec_out[row_dim] *= slab_in.shape[0]
+    s_next = jnp.moveaxis(slab_in, 0, row_dim).reshape(vec_out)
+    return s_next
+
+
+def guide_masks(u, group_axis):
+    total_devices = lax.axis_size(group_axis)
+    g_now = u[None]
+    for d in range(total_devices.bit_length() - 1):
+        parts_out = 1 << d
+        r2 = lax.ppermute(g_now, group_axis, [(m, m ^ parts_out) for m in range(total_devices)])
+        step_out = jnp.stack([g_now, r2], axis=0)
+        carry_in = lax.axis_index(group_axis)
+        local_out = carry_in >> d & 1
+        g_now = jnp.where(local_out == 0, step_out, step_out[::-1]).reshape(-1, *u.shape)
+    return g_now
+
+
+def cover_the_rounds(xs, x_local, d_out):
+    item_now = guide_masks(xs, x_local)
+    built = fix_levels_all(item_now, d_out)
+    return built
+
+
+choose_indices_up = functools.partial(cover_the_rounds, x_local=("fsdp", "dp"), d_out=0)
 
 
 def extended(array, sides, width):
@@ -116,7 +146,7 @@
         lax.all_gather(query_in, ("fsdp", "dp"), axis=0, tiled=True),
         lax.all_gather(query_out, ("fsdp", "dp"), axis=0, tiled=True),
         lax.all_gather(value_in, ("fsdp", "dp"), axis=0, tiled=True),
-        lax.all_gather(value_out, ("fsdp", "dp"), axis=0, tiled=True),
+        choose_indices_up(value_out),
         lax.all_gather(up_in, ("fsdp", "dp"), axis=0, tiled=True),
         lax.all_gather(up_out, ("fsdp", "dp"), axis=0, tiled=True),
         lax.all_gather(down_in, ("fsdp", "dp"), axis=0, tiled=True),

time: 2060 us -> 2010 us (0.976)
  waiting for transfers between devices: 908 us -> 769 us
  blocking collectives: 519 us -> 602 us
    all_gather x1, blocking collectives: 70.7 us -> 143 us  [local(): lax.all_gather(value_out, ('fsdp', 'dp'), axis=0, tiled=True)]
    reduce_scatter x1, waiting for transfers between devices: 135 us -> 84.1 us  [local(): lax.psum_scatter(grad_query_out, ('fsdp', 'dp'), scatter_dimension=0, til...]
    ppermute x2, waiting for transfers between devices: 48.8 us -> 0.01 us  [from_behind(): lax.ppermute(value, axis, [(source, source + steps) for source in range(f...]
    unnamed x17, waiting for transfers between devices: 46.4 us -> 4.48 us
  transfers between devices with their start and end apart: 20 -> 25, of which waited for: 9 -> 7; matrix products, arithmetic and copies ran while one was open for 20% -> 21% of each run, Pallas kernels for 0% -> 0%
where the time goes in v1:
time: 2010 us; the launch traced here: 2000 us
  waiting for transfers between devices  769 us (38%)
  blocking collectives  602 us (30%)
  matrix products  376 us (19%)
  other arithmetic  141 us (7%)
  local copies, waits for them, and re-layouts  83.4 us (4%)
    all_gather x1, blocking collectives, local(): lax.all_gather(down_out, ('fsdp', 'dp'), axis=0, tiled=True)  177 us
    all_gather x1, blocking collectives, local(): lax.all_gather(value_out, ('fsdp', 'dp'), axis=0, tiled=True)  143 us
    reduce_scatter x1, waiting for transfers between devices, local(): lax.psum_scatter(grad_down_in, ('fsdp', 'dp'), scatter_dimension=0, tiled...  137 us
    reduce_scatter x1, waiting for transfers between devices, local(): lax.psum_scatter(grad_up_out, ('fsdp', 'dp'), scatter_dimension=0, tiled=...  137 us
    reduce_scatter x1, waiting for transfers between devices, local(): lax.psum_scatter(grad_value_in, ('fsdp', 'dp'), scatter_dimension=0, tile...  134 us
    reduce_scatter x1, waiting for transfers between devices, local(): lax.psum_scatter(grad_value_out, ('fsdp', 'dp'), scatter_dimension=0, til...  134 us
    reduce_scatter x1, waiting for transfers between devices, local(): lax.psum_scatter(grad_query_in, ('fsdp', 'dp'), scatter_dimension=0, tile...  134 us
    reduce_scatter x1, waiting for transfers between devices, local(): lax.psum_scatter(grad_query_out, ('fsdp', 'dp'), scatter_dimension=0, til...  84.1 us
  transfers between devices with their start and end apart: 25, of which 7 were waited for; matrix products, arithmetic and copies ran while one was open for 21% of the time, Pallas kernels for 0%

profile of v1, /device:TPU:0, one launch (start us, length us, event | category | flops | bytes accessed | tf_op | source)
XLA Modules:
  0.0 2002.4 jit_solution(12745363326962083792)
XLA Ops:
  19.4 69.7 %all_gather.57 = bf16[1024,128]{1,0:T(8,128)(2,1)S(1)} all-gather(bf16[32,128]{1,0:T(8,128)(2,1)S(1)} %copy-done.94), channel_id=1, replica_groups=mesh['fsdp'=16,'dp'=2] {'fsdp','dp'}, dimensions={0}, use_global_device_ids=true | all-gather | bytes 270336 | tf_op jit(solution)/shard_map/all_gather | solution.py:148
  93.4 70.1 %all_gather.59 = bf16[1024,128]{1,0:T(8,128)(2,1)} all-gather(bf16[32,128]{1,0:T(8,128)(2,1)S(1)} %copy-done.95), channel_id=1, replica_groups=mesh['fsdp'=16,'dp'=2] {'fsdp','dp'}, dimensions={0}, use_global_device_ids=true | all-gather | bytes 270336 | tf_op jit(solution)/shard_map/all_gather | solution.py:146
  163.7 72.1 %all_gather.60 = bf16[1024,128]{1,0:T(8,128)(2,1)} all-gather(bf16[32,128]{1,0:T(8,128)(2,1)S(1)} %copy-done.96), channel_id=1, replica_groups=mesh['fsdp'=16,'dp'=2] {'fsdp','dp'}, dimensions={0}, use_global_device_ids=true | all-gather | bytes 270336 | tf_op jit(solution)/shard_map/all_gather | solution.py:147
  235.8 70.9 %all_gather.63 = bf16[1024,128]{1,0:T(8,128)(2,1)} all-gather(bf16[32,128]{1,0:T(8,128)(2,1)S(1)} %copy-done.97), channel_id=1, replica_groups=mesh['fsdp'=16,'dp'=2] {'fsdp','dp'}, dimensions={0}, use_global_device_ids=true | all-gather | bytes 270336 | tf_op jit(solution)/shard_map/all_gather | solution.py:150
  315.6 6.2 fusion.40
  328.6 176.9 %all_gather.67 = bf16[1024,128]{1,0:T(8,128)(2,1)S(1)} all-gather(bf16[32,128]{1,0:T(8,128)(2,1)S(1)} %copy-done.98), channel_id=1, replica_groups=mesh['fsdp'=16,'dp'=2] {'fsdp','dp'}, dimensions={0}, use_global_device_ids=true | all-gather | bytes 270336 | tf_op jit(solution)/shard_map/all_gather | solution.py:153
  545.0 11.7 fusion.92
  556.8 10.2 fusion.1
  567.6 10.1 fusion.53
  577.7 10.3 fusion.91
  588.0 10.1 fusion.2
  598.7 11.0 fusion.52
  609.8 10.5 fusion.90
  620.3 10.1 fusion.3
  631.0 10.8 fusion.51
  641.8 10.4 fusion.93
  652.2 10.1 fusion
  663.0 11.0 fusion.54
  682.1 12.1 fusion.99
  694.3 12.2 fusion.97
  706.4 13.5 multiply_convert_fusion.5
  719.9 11.2 multiply_convert_fusion.4
  735.2 11.0 fusion.100
  751.8 11.1 fusion.8
  762.9 18.6 multiply_reduce_fusion
  781.5 15.7 multiply_convert_fusion
  803.7 11.2 fusion.10
  814.9 18.9 multiply_reduce_fusion.1
  834.0 11.1 fusion.12
  845.1 18.6 multiply_reduce_fusion.2
  863.9 11.2 fusion.14
  875.1 18.6 multiply_reduce_fusion.3
  907.5 15.8 multiply_convert_fusion.1
  929.5 15.7 multiply_convert_fusion.2
  951.3 15.7 multiply_convert_fusion.3
  986.9 9.8 convert.60
  1012.3 8.0 fusion.57
  1020.4 8.1 fusion.56
  1028.6 8.1 fusion.55
  1038.2 142.8 %all_gather.68 = bf16[1024,128]{1,0:T(8,128)(2,1)} all-gather(bf16[32,128]{1,0:T(8,128)(2,1)S(1)} %copy-done.90), channel_id=1, replica_groups=mesh['fsdp'=16,'dp'=2] {'fsdp','dp'}, dimensions={0}, use_global_device_ids=true | all-gather | bytes 270336 | tf_op jit(solution)/shard_map/all_gather | solution.py:234
  1195.8 6.1 fusion.106
  1208.3 11.0 fusion.98
  1234.1 84.1 %reduce-scatter.13.cloned.1.call-done = f32[32,128]{1,0:T(8,128)} async-done(((f32[1024,128]{1,0:T(8,128)}), f32[32,128]{1,0:T(8,128)}) %reduce-scatter.13.cloned.1.call-update) | async-done | bytes 16400 | tf_op jit(solution)/shard_map/reduce_scatter | solution.py:332
  1318.2 134.3 %reduce-scatter.11.cloned.1.call-done = f32[32,128]{1,0:T(8,128)} async-done(((f32[1024,128]{1,0:T(8,128)}), f32[32,128]{1,0:T(8,128)}) %reduce-scatter.11.cloned.1.call-update) | async-done | bytes 16400 | tf_op jit(solution)/shard_map/reduce_scatter | solution.py:331
  1452.5 134.5 %reduce-scatter.15.cloned.1.call-done = f32[32,128]{1,0:T(8,128)} async-done(((f32[1024,128]{1,0:T(8,128)}), f32[32,128]{1,0:T(8,128)}) %reduce-scatter.15.cloned.1.call-update) | async-done | bytes 16400 | tf_op jit(solution)/shard_map/reduce_scatter | solution.py:333
  1587.0 134.4 %reduce-scatter.17.cloned.1.call-done = f32[32,128]{1,0:T(8,128)} async-done(((f32[1024,128]{1,0:T(8,128)}), f32[32,128]{1,0:T(8,128)}) %reduce-scatter.17.cloned.1.call-update) | async-done | bytes 16400 | tf_op jit(solution)/shard_map/reduce_scatter | solution.py:334
  1721.4 136.7 %reduce-scatter.21.cloned.1.call-done = f32[128,128]{1,0:T(8,128)} async-done(((f32[4096,128]{1,0:T(8,128)}), f32[128,128]{1,0:T(8,128)}) %reduce-scatter.21.cloned.1.call-update) | async-done | bytes 65552 | tf_op jit(solution)/shard_map/reduce_scatter | solution.py:336
  1858.0 137.5 %reduce-scatter.23.cloned.1.call-done = f32[128,128]{1,0:T(8,128)} async-done(((f32[4096,128]{1,0:T(8,128)}), f32[128,128]{1,0:T(8,128)}) %reduce-scatter.23.cloned.1.call-update) | async-done | bytes 65552 | tf_op jit(solution)/shard_map/reduce_scatter | solution.py:337
  (389 shorter events, 196.9 us)
Async XLA Ops:
  7.2 300.2 %all-gather.11.cloned.1.call-start = ((), (), s32[]{:S(2)}) async-start(), calls=%async_computation.9 | async-start | bytes 2162688 | tf_op jit(solution)/shard_map/all_gather | solution.py:142
  7.9 303.6 %all-gather.9.cloned.1.call-start = ((), (), s32[]{:S(2)}) async-start(), calls=%async_computation.8 | async-start | bytes 2162688 | tf_op jit(solution)/shard_map/all_gather | solution.py:141
  8.7 500.3 %all-gather.13.cloned.1.call-start = ((), (), s32[]{:S(2)}) async-start(), calls=%async_computation.10 | async-start | bytes 2162688 | tf_op jit(solution)/shard_map/all_gather | solution.py:140
  9.4 664.5 %all-gather.15.cloned.1.call-start = ((), (), s32[]{:S(2)}) async-start(), calls=%async_computation.11 | async-start | bytes 2162688 | tf_op jit(solution)/shard_map/all_gather | solution.py:143
  10.0 672.1 %all-gather.21.cloned.1.call-start = ((), (), s32[]{:S(2)}) async-start(), calls=%async_computation.14 | async-start | bytes 8650752 | tf_op jit(solution)/shard_map/all_gather | solution.py:145
  10.6 683.7 %all-gather.17.cloned.1.call-start = ((), (), s32[]{:S(2)}) async-start(), calls=%async_computation.12 | async-start | bytes 8650752 | tf_op jit(solution)/shard_map/all_gather | solution.py:144
  11.2 695.3 %all-gather.19.cloned.1.call-start = ((), (), s32[]{:S(2)}) async-start(), calls=%async_computation.13 | async-start | bytes 1081344 | tf_op jit(solution)/shard_map/all_gather | solution.py:151
  11.9 708.0 %all-gather.23.cloned.1.call-start = ((), (), s32[]{:S(2)}) async-start(), calls=%async_computation.15 | async-start | bytes 1081344 | tf_op jit(solution)/shard_map/all_gather | solution.py:152
  12.0 7.3 collective-permute-start
  15.0 1219.0 %reduce-scatter.19.cloned.1.call-start = ((), (), s32[]{:S(2)}) async-start(), calls=%async_computation.20 | async-start | bytes 540672 | tf_op jit(solution)/shard_map/reduce_scatter | solution.py:335
  16.8 72.2 %copy-start.85 = (f32[768]{0:T(1024)}, f32[768]{0:T(1024)S(1)}, u32[]{:S(2)}) copy-start(f32[768]{0:T(1024)S(1)} %broadcast_multiply_fusion.5) | copy-start | bytes 9220
  17.4 71.7 %copy-start.87 = (f32[768]{0:T(1024)}, f32[768]{0:T(1024)S(1)}, u32[]{:S(2)}) copy-start(f32[768]{0:T(1024)S(1)} %add_rsqrt_fusion.1) | copy-start | bytes 9220
  18.2 75.2 %copy-start.95 = (bf16[32,128]{1,0:T(8,128)(2,1)S(1)}, bf16[32,128]{1,0:T(8,128)(2,1)}, u32[]{:S(2)}) copy-start(bf16[32,128]{1,0:T(8,128)(2,1)} %param.46) | copy-start | bytes 24580
  18.9 490.1 %copy-start.7 = (bf16[768,1024]{1,0:T(8,128)(2,1)}, bf16[768,1024]{1,0:T(8,128)(2,1)S(1)}, u32[]{:S(2)}) copy-start(bf16[768,1024]{1,0:T(8,128)(2,1)S(1)} %fusion.32) | copy-start | bytes 4718596
  18.9 144.8 %copy-start.96 = (bf16[32,128]{1,0:T(8,128)(2,1)S(1)}, bf16[32,128]{1,0:T(8,128)(2,1)}, u32[]{:S(2)}) copy-start(bf16[32,128]{1,0:T(8,128)(2,1)} %param.47) | copy-start | bytes 24580
  18.9 216.9 %copy-start.97 = (bf16[32,128]{1,0:T(8,128)(2,1)S(1)}, bf16[32,128]{1,0:T(8,128)(2,1)}, u32[]{:S(2)}) copy-start(bf16[32,128]{1,0:T(8,128)(2,1)} %param.50) | copy-start | bytes 24580
  19.3 70.0 %collective-permute-start.1 = (bf16[2,32,128]{2,1,0:T(8,128)(2,1)S(1)}, bf16[2,32,128]{2,1,0:T(8,128)(2,1)S(1)}, u32[]{:S(2)}, u32[]{:S(2)}) collective-permute-start(bf16[2,32,128]{2,1,0:T(8,128)(2,1)S(1)} %get-tuple-element.65), channel_id=1, source_target_pairs={{0,2},{1,3},{2,0},{3,1},{4,6},{5,7},{6,4},{7,5},{8,10},{9,11},{10,... | collective-permute-start | bytes 49160 | tf_op jit(solution)/shard_map/ppermute | solution.py:27
  89.1 221.8 %copy-start.55 = (bf16[1024,128]{1,0:T(8,128)(2,1)}, bf16[1024,128]{1,0:T(8,128)(2,1)S(1)}, u32[]{:S(2)}) copy-start(bf16[1024,128]{1,0:T(8,128)(2,1)S(1)} %all_gather.57) | copy-start | bytes 786436
  89.3 417.5 %copy-start.45 = (bf16[768,128]{1,0:T(8,128)(2,1)}, bf16[768,128]{1,0:T(8,128)(2,1)S(1)}, u32[]{:S(2)}) copy-start(bf16[768,128]{1,0:T(8,128)(2,1)S(1)} %copy.96) | copy-start | bytes 589828
  89.3 4.0 collective-permute-start.2
  90.0 220.9 %copy-start.70 = (bf16[768,128]{1,0:T(8,128)(2,1)}, bf16[768,128]{1,0:T(8,128)(2,1)S(1)}, u32[]{:S(2)}) copy-start(bf16[768,128]{1,0:T(8,128)(2,1)S(1)} %fusion.67) | copy-start | bytes 589828
  93.3 70.2 %collective-permute-start.3 = (bf16[8,32,128]{2,1,0:T(8,128)(2,1)S(1)}, bf16[8,32,128]{2,1,0:T(8,128)(2,1)S(1)}, u32[]{:S(2)}, u32[]{:S(2)}) collective-permute-start(bf16[8,32,128]{2,1,0:T(8,128)(2,1)S(1)} %bitcast.245), channel_id=1, source_target_pairs={{0,8},{1,9},{2,10},{3,11},{4,12},{5,13},{6,14},{7,15},{8,0},{9,1},... | collective-permute-start | bytes 196616 | tf_op jit(solution)/shard_map/ppermute | solution.py:27
  163.6 143.0 %collective-permute-start.4 = (bf16[16,32,128]{2,1,0:T(8,128)(2,1)S(1)}, bf16[16,32,128]{2,1,0:T(8,128)(2,1)S(1)}, u32[]{:S(2)}, u32[]{:S(2)}) collective-permute-start(bf16[16,32,128]{2,1,0:T(8,128)(2,1)S(1)} %bitcast.243), channel_id=1, source_target_pairs={{0,16},{1,17},{2,18},{3,19},{4,20},{5,21},{6,22},{7,23},{8,24},{9,... | collective-permute-start | bytes 393224 | tf_op jit(solution)/shard_map/ppermute | solution.py:27
  315.5 13.1 copy-start.98
  315.5 189.9 %copy-start.57 = (bf16[1024,128]{1,0:T(8,128)(2,1)S(1)}, bf16[1024,128]{1,0:T(8,128)(2,1)}, u32[]{:S(2)}) copy-start(bf16[1024,128]{1,0:T(8,128)(2,1)} %all_gather.59) | copy-start | bytes 786436
  315.6 191.2 %copy-start.19 = (bf16[768,1024]{1,0:T(8,128)(2,1)S(1)}, bf16[768,1024]{1,0:T(8,128)(2,1)}, u32[]{:S(2)}) copy-start(bf16[768,1024]{1,0:T(8,128)(2,1)} %param.28) | copy-start | bytes 4718596
  321.8 199.0 %collective-permute-start.5 = (bf16[576,2048]{1,0:T(8,128)(2,1)}, bf16[576,2048]{1,0:T(8,128)(2,1)}, u32[]{:S(2)}, u32[]{:S(2)}) collective-permute-start(bf16[576,2048]{1,0:T(8,128)(2,1)} %get-tuple-element.54), channel_id=1, source_target_pairs={{0,1},{1,2},{2,3},{3,4},{4,5},{5,6},{6,7},{7,8},{8,9},{9,10},{10,1... | collective-permute-start | bytes 7077896 | tf_op jit(solution)/shard_map/ppermute | solution.py:51
  327.2 193.6 %collective-permute-start.6 = (bf16[576,2048]{1,0:T(8,128)(2,1)}, bf16[576,2048]{1,0:T(8,128)(2,1)}, u32[]{:S(2)}, u32[]{:S(2)}) collective-permute-start(bf16[576,2048]{1,0:T(8,128)(2,1)} %get-tuple-element.55), channel_id=1, source_target_pairs={{1,0},{2,1},{3,2},{4,3},{5,4},{6,5},{7,6},{8,7},{9,8},{10,9},{11,1... | collective-permute-start | bytes 7077896 | tf_op jit(solution)/shard_map/ppermute | solution.py:52
  530.1 111.7 %copy-start.9 = (bf16[1920,256]{0,1:T(8,128)(2,1)}, bf16[1920,256]{0,1:T(8,128)(2,1)S(1)}, u32[]{:S(2)}) copy-start(bf16[1920,256]{0,1:T(8,128)(2,1)S(1)} %copy.100) | copy-start | bytes 2949124
  540.2 16.6 copy-start.11
  678.4 69.1 %copy-start.3 = (f32[768,1024]{1,0:T(8,128)}, f32[768,1024]{1,0:T(8,128)S(1)}, u32[]{:S(2)}) copy-start(f32[768,1024]{1,0:T(8,128)S(1)} %get-tuple-element.75) | copy-start | bytes 9437188
  706.4 13.5 copy-start.74
  781.5 15.7 copy-start.16
  814.9 19.1 copy-start.79
  845.1 18.8 copy-start.80
  893.7 340.4 %reduce-scatter.25.cloned.1.call-start = ((), (), s32[]{:S(2)}) async-start(), calls=%async_computation.23 | async-start | bytes 540672
  907.5 15.8 copy-start.52
  929.5 15.7 copy-start.50
  951.3 15.8 copy-start.49
  1008.2 176.1 %collective-permute-start.7 = (bf16[576,2048]{1,0:T(8,128)(2,1)}, bf16[576,2048]{1,0:T(8,128)(2,1)}, u32[]{:S(2)}, u32[]{:S(2)}) collective-permute-start(bf16[576,2048]{1,0:T(8,128)(2,1)} %get-tuple-element.44), channel_id=1, source_target_pairs={{0,1},{1,2},{2,3},{3,4},{4,5},{5,6},{6,7},{7,8},{8,9},{9,10},{10,1... | collective-permute-start | bytes 7077896 | tf_op jit(solution)/shard_map/ppermute | solution.py:60
  1010.9 173.4 %collective-permute-start.8 = (bf16[576,2048]{1,0:T(8,128)(2,1)}, bf16[576,2048]{1,0:T(8,128)(2,1)}, u32[]{:S(2)}, u32[]{:S(2)}) collective-permute-start(bf16[576,2048]{1,0:T(8,128)(2,1)} %get-tuple-element.45), channel_id=1, source_target_pairs={{1,0},{2,1},{3,2},{4,3},{5,4},{6,5},{7,6},{8,7},{9,8},{10,9},{11,1... | collective-permute-start | bytes 7077896 | tf_op jit(solution)/shard_map/ppermute | solution.py:60
  1020.4 297.8 %reduce-scatter.13.cloned.1.call-start = ((), (), s32[]{:S(2)}) async-start(), calls=%async_computation.17 | async-start | bytes 540672 | tf_op jit(solution)/shard_map/reduce_scatter | solution.py:332
  1036.7 144.3 %copy-start.66 = (bf16[1024,128]{1,0:T(8,128)(2,1)S(1)}, bf16[1024,128]{1,0:T(8,128)(2,1)}, u32[]{:S(2)}) copy-start(bf16[1024,128]{1,0:T(8,128)(2,1)} %all_gather.60) | copy-start | bytes 786436
  1038.1 414.4 %reduce-scatter.11.cloned.1.call-start = ((), (), s32[]{:S(2)}) async-start(), calls=%async_computation.16 | async-start | bytes 540672 | tf_op jit(solution)/shard_map/reduce_scatter | solution.py:331
  1184.2 402.8 %reduce-scatter.15.cloned.1.call-start = ((), (), s32[]{:S(2)}) async-start(), calls=%async_computation.18 | async-start | bytes 540672 | tf_op jit(solution)/shard_map/reduce_scatter | solution.py:333
  1192.8 528.5 %reduce-scatter.17.cloned.1.call-start = ((), (), s32[]{:S(2)}) async-start(), calls=%async_computation.19 | async-start | bytes 540672 | tf_op jit(solution)/shard_map/reduce_scatter | solution.py:334
  1195.8 662.2 %reduce-scatter.21.cloned.1.call-start = ((), (), s32[]{:S(2)}) async-start(), calls=%async_computation.21 | async-start | bytes 2162688 | tf_op jit(solution)/shard_map/reduce_scatter | solution.py:336
  1201.9 793.6 %reduce-scatter.23.cloned.1.call-start = ((), (), s32[]{:S(2)}) async-start(), calls=%async_computation.22 | async-start | bytes 2162688 | tf_op jit(solution)/shard_map/reduce_scatter | solution.py:337
  (88 other events, 463.2 us)
Sparse Core Ops, SparseCore 0:
  11.1 59.5 all-gather.10
  73.8 55.5 all-gather.8
  132.5 57.0 all-gather.12
  192.6 55.6 all-gather.14
  251.2 107.1 all-gather.20
  361.3 86.7 all-gather.16
  451.0 52.3 all-gather.18
  506.2 52.7 all-gather.22
  893.8 149.0 reduce-scatter.18
  1045.6 137.7 reduce-scatter.24
  1186.1 131.9 reduce-scatter.12
  1320.8 131.6 reduce-scatter.10
  1455.3 131.6 reduce-scatter.14
  1589.6 131.6 reduce-scatter.16
  1724.0 133.9 reduce-scatter.20
  1860.7 134.7 reduce-scatter.22
